TPU v7x, 32 devices: a whole 2x2x4 slice. The times are simulated.
32 devices in a mesh: row: 8 (over z, x), col: 4 (over y, core).
Axes of the slice: x: 2, y: 2, z: 4, core: 2. Of those that a mesh axis runs over, the one named last changes fastest.
Arguments:
- krylov_block: bfloat16 [64, 16384], P(None, ('row', 'col')), may hold values from -54 to 54
- degree: int32 [16384], P(('row', 'col')), may hold values from 16 to 64
- tile_values: bfloat16 [256, 4, 64, 512], P('row', 'col'), may hold values from -6 to 6
- tile_column: int32 [256, 4, 8], P('row', 'col'), may hold values from 0 to 63
- tile_live: int32 [256, 4, 8], P('row', 'col'), may hold values 0 or 1
Outputs:
- orthonormal: float32 [64, 16384], P(None, ('row', 'col'))
- quotient: float32 [64, 64], replicated
All inputs are finite; a program needn't handle non-finite values. No bound on the sum of `tile_live` on one device may be relied on, other than what follows from the above.
Results may differ from a plain program's by a relative error of at most 0.0032.
Values may be sent and summed in bfloat16 or wider, within the bound.
No kernel may reach another device: no remote copies, remote signals or barrier semaphores. Data moves between devices by JAX's collectives and lax.ppermute only.
A program may use at most 128 MiB of HBM per device.

v0:
```python
import math
import jax
import jax.numpy as jnp
from jax import lax
from jax.sharding import PartitionSpec as P


def gram_of(left, right):
    return lax.dot_general(
        left,
        right,
        (((1,), (1,)), ((), ())),
        precision=lax.Precision.HIGHEST,
        preferred_element_type=jnp.float32,
    )


def on_device(krylov_block, degree, tile_values, tile_column, tile_live):
    vectors = krylov_block.shape[0]
    owned_rows = krylov_block.shape[1]
    block_rows = tile_values.shape[0]
    height = tile_values.shape[2]
    slot_width = tile_values.shape[3]
    sources = lax.axis_size("row")
    groups = lax.axis_size("col")
    per_piece = owned_rows // height
    inv_root = lax.rsqrt(degree.astype(jnp.float32))
    basis_wide = krylov_block.astype(jnp.float32)
    scaled = (basis_wide * inv_root[None, :]).astype(jnp.bfloat16)
    gathered = lax.all_gather(scaled, "row", axis=1, tiled=True)
    blocks = gathered.reshape(vectors, sources * per_piece, height)
    pick_index = tile_column[:, 0, :].reshape(-1)
    chosen = jnp.take(blocks, pick_index, axis=1)
    chosen = chosen * tile_live[:, 0, :].reshape(1, -1, 1).astype(jnp.bfloat16)
    chosen = chosen.reshape(vectors, block_rows, slot_width)
    panel = tile_values[:, 0]
    whole_rows = jnp.einsum("klc,luc->klu", chosen, panel, preferred_element_type=jnp.float32)
    whole_rows = whole_rows.reshape(vectors, block_rows * height)
    spread = lax.psum_scatter(whole_rows, "col", scatter_dimension=1, tiled=True)
    applied = basis_wide - inv_root[None, :] * spread
    quotient, energy = lax.psum(
        (gram_of(basis_wide, applied), gram_of(applied, applied)), ("row", "col")
    )
    factor = jnp.linalg.cholesky(energy)
    identity = jnp.eye(vectors, dtype=jnp.float32)
    inverse = lax.linalg.triangular_solve(factor, identity, left_side=True, lower=True)
    total_rows = sources * groups * owned_rows
    orthonormal = jnp.dot(inverse, applied, precision=lax.Precision.HIGHEST) * math.sqrt(total_rows)
    return (orthonormal, quotient / total_rows)


def solution(mesh):
    return jax.shard_map(
        on_device,
        mesh=mesh,
        in_specs=(
            P(None, ("row", "col")),
            P(("row", "col")),
            P("row", "col", None, None),
            P("row", "col", None),
            P("row", "col", None),
        ),
        out_specs=(P(None, ("row", "col")), P()),
        check_vma=False,
    )
```

profile of v0, /device:TPU:0, one launch (start us, length us, event | category | flops | bytes accessed | tf_op | source)
XLA Modules:
  0.0 156.6 jit_solution(8631686106743871151)
XLA Ops:
  7.2 0.9 copy.22
  8.1 0.7 compare_and_fusion
  8.8 0.7 convert_rsqrt_fusion
  9.5 0.9 fusion.8
  10.4 33.0 %all_gather.3 = bf16[64,4096]{1,0:T(8,128)(2,1)S(1)} all-gather(bf16[64,512]{1,0:T(8,128)(2,1)S(1)} %fusion.8), channel_id=1, replica_groups=mesh['row'=8,'col'=4] {'row'}, dimensions={1}, use_global_device_ids=true | all-gather | bytes 589824 | tf_op jit(solution)/shard_map/all_gather | solution.py:30
  43.4 2.1 %reshape.72 = bf16[64,64,64]{2,1,0:T(8,128)(2,1)} reshape(bf16[64,4096]{1,0:T(8,128)(2,1)S(1)} %all_gather.3) | data formatting | bytes 1048576 | tf_op jit(solution)/shard_map/reshape | solution.py:31
  45.5 1.9 %copy.23 = bf16[64,64,64]{2,0,1:T(8,128)(2,1)S(1)} copy(bf16[64,64,64]{2,1,0:T(8,128)(2,1)} %reshape.72) | data formatting | bytes 1048576 | tf_op jit(solution)/shard_map/reshape | solution.py:31
  47.4 0.1 reshape_squeeze.7
  47.5 3.1 %gather_fusion = bf16[256,64,64]{2,1,0:T(8,128)(2,1)} fusion(bf16[64,64,64]{2,0,1:T(8,128)(2,1)S(1)} %copy.23, s32[1024]{0:T(1024)S(1)} %pad_clamp_fusion), kind=kCustom, calls=%fused_computation | custom fusion | bytes 4195328 | tf_op jit(solution)/shard_map/jit(_take)/gather | solution.py:33
  50.6 6.8 %copy.24 = bf16[64,256,64]{2,1,0:T(8,128)(2,1)} copy(bf16[64,256,64]{2,0,1:T(8,128)(2,1)} %bitcast.30) | data formatting | bytes 4194304 | tf_op jit(solution)/shard_map/jit(_take)/gather | solution.py:33
  57.4 6.5 %gather.7 = bf16[64,32,512]{2,1,0:T(8,128)(2,1)} reshape(bf16[64,256,64]{2,1,0:T(8,128)(2,1)} %copy.24) | data formatting | bytes 4194304 | tf_op jit(solution)/shard_map/jit(_take)/gather | solution.py:33
  63.9 0.1 copy.25
  64.0 0.1 mul.35
  64.1 0.1 mul.36
  64.2 0.1 copy.21
  64.3 0.1 broadcast_in_dim.18
  64.4 0.1 broadcast_in_dim.19
  64.5 1.8 %select_multiply_fusion = bf16[64,32,512]{2,1,0:T(8,128)(2,1)S(1)} fusion(bf16[64,32,512]{2,1,0:T(8,128)(2,1)} %gather.7, pred[32,512]{1,0:T(8,128)(4,1)S(1)} %broadcast_in_dim.19, bf16[32,512]{1,0:T(8,128)(2,1)S(1)} %mul.36), kind=kLoop, calls=%fused_computation.4 | loop fusion | flops 2097152 | bytes 4243456 | tf_op jit(solution)/shard_map/mul | solution.py:34
  66.3 1.4 fusion.3
  67.7 0.6 copy.27
  68.4 1.1 reshape.73
  69.5 22.9 %reduce-scatter.2.cloned.1.call-done = f32[64,512]{1,0:T(8,128)} async-done(((f32[64,2048]{1,0:T(8,128)}), f32[64,512]{1,0:T(8,128)}) %reduce-scatter.2.cloned.1.call-update) | async-done | bytes 131088 | tf_op jit(solution)/shard_map/reduce_scatter | solution.py:39
  92.5 1.1 convolution_bitcast_fusion
  93.6 1.3 fusion.9
  94.8 40.0 %all-reduce = (f32[64,64]{0,1:T(8,128)S(1)}, f32[64,64]{0,1:T(8,128)S(1)}) all-reduce(f32[64,64]{0,1:T(8,128)S(1)} %fusion.9, f32[64,64]{0,1:T(8,128)S(1)} %convolution_bitcast_fusion), channel_id=1, replica_groups=mesh['row'=8,'col'=4] {'row','col'}, use_global_device_ids=true, to_apply=%region_1.2 | all-reduce | flops 8192 | bytes 65536 | tf_op jit(solution)/shard_map/psum | solution.py:41
  134.9 5.8 %cholesky.17 = f32[64,64]{1,0:T(8,128)S(1)} custom-call(f32[64,64]{1,0:T(8,128)S(1)} %fusion.16), custom_call_target="Cholesky" | custom-call | tf_op jit(solution)/shard_map/jit(cholesky)/cholesky | solution.py:44
  140.8 0.6 compare_reduce_fusion
  141.4 0.7 fusion.13
  142.1 4.9 %custom-call.6 = f32[1,64,64]{1,2,0:T(8,128)S(1)} custom-call(f32[1,64,64]{2,1,0:T(8,128)S(1)} %fusion.13), custom_call_target="InvertDiagBlocksLowerTriangular" | custom-call | tf_op jit(solution)/shard_map/triangular_solve | solution.py:46
  147.0 0.2 fusion.14
  147.3 0.7 copy.30
  148.0 1.8 %convolution_multiply_fusion = f32[64,512]{1,0:T(8,128)} fusion(f32[64,64]{1,0:T(8,128)S(1)} %fusion.14, bf16[64,512]{1,0:T(8,128)(2,1)S(1)} %copy-done.1, f32[64,512]{1,0:T(8,128)} %reduce-scatter.2.cloned.1.call-done, f32[512]{0:T(512)S(1)} %convert_rsqrt_fusion), kind=kOutput, calls=%fused_computation.6 | convolution fusion | flops 25296896 | bytes 346112 | tf_op jit(solution)/shard_map/dot_general | solution.py:48
  (15 shorter events, 0.2 us)
Async XLA Ops:
  7.2 59.1 %copy-start = (bf16[32,1,64,512]{3,2,1,0:T(8,128)(2,1)S(1)}, bf16[32,1,64,512]{3,2,1,0:T(8,128)(2,1)}, u32[]{:S(2)}) copy-start(bf16[32,1,64,512]{3,2,1,0:T(8,128)(2,1)} %param.7) | copy-start | bytes 6291460
  7.2 85.3 %reduce-scatter.2.cloned.1.call-start = ((), (), s32[]{:S(2)}) async-start(), calls=%async_computation.1 | async-start | bytes 655360 | tf_op jit(solution)/shard_map/reduce_scatter | solution.py:39
  57.4 6.5 %copy-start.2 = (s32[32,1,8]{0,2,1:T(8,128)S(1)}, s32[32,1,8]{0,2,1:T(8,128)}, u32[]{:S(2)}) copy-start(s32[32,1,8]{0,2,1:T(8,128)} %param.9) | copy-start | bytes 3076
  67.7 24.7 %copy-start.1 = (bf16[64,512]{1,0:T(8,128)(2,1)S(1)}, bf16[64,512]{1,0:T(8,128)(2,1)}, u32[]{:S(2)}) copy-start(bf16[64,512]{1,0:T(8,128)(2,1)} %param.5) | copy-start | bytes 196612
Sparse Core Ops, SparseCore 0:
  69.7 22.7 reduce-scatter.1
where the time goes:
time: 157 us
  blocking collectives  73 us (46%)
  local copies, waits for them, and re-layouts  24.5 us (16%)
  waiting for transfers between devices  22.9 us (15%)
  other arithmetic  16.1 us (10%)
  between operations  14.1 us (9%)
  matrix products  5.85 us (4%)
    psum x1, blocking collectives, on_device(): lax.psum((gram_of(basis_wide, applied), gram_of(applied, applied)), ('row...  40 us
    all_gather x1, blocking collectives, on_device(): gathered = lax.all_gather(scaled, 'row', axis=1, tiled=True)  33 us
    reduce_scatter x1, waiting for transfers between devices, on_device(): lax.psum_scatter(whole_rows, 'col', scatter_dimension=1, tiled=True)  22.9 us
    gather x3, local copies, waits for them, and re-layouts, on_device(): chosen = jnp.take(blocks, pick_index, axis=1)  16.3 us
    another operation x3, other arithmetic, on_device(): factor = jnp.linalg.cholesky(energy)  6.52 us
    another operation x2, other arithmetic, on_device(): lax.linalg.triangular_solve(factor, identity, left_side=True, lower=True)  5.55 us
    reshape x2, local copies, waits for them, and re-layouts, on_device(): blocks = gathered.reshape(vectors, sources * per_piece, height)  4.01 us
  transfers between devices with their start and end apart: 1, of which 1 were waited for; matrix products, arithmetic and copies ran while one was open for 0% of the time, Pallas kernels for 0%

commit v1 on v0

--- a/solution.py
+++ b/solution.py
@@ -3,6 +3,11 @@
 import jax.numpy as jnp
 from jax import lax
 from jax.sharding import PartitionSpec as P
+
+
+def by_each_axis(value, axis_one, axis_two):
+    half = lax.psum(value, axis_one)
+    return lax.psum(half, axis_two)
 
 
 def gram_of(left, right):
@@ -38,8 +43,8 @@
     whole_rows = whole_rows.reshape(vectors, block_rows * height)
     spread = lax.psum_scatter(whole_rows, "col", scatter_dimension=1, tiled=True)
     applied = basis_wide - inv_root[None, :] * spread
-    quotient, energy = lax.psum(
-        (gram_of(basis_wide, applied), gram_of(applied, applied)), ("row", "col")
+    quotient, energy = by_each_axis(
+        (gram_of(basis_wide, applied), gram_of(applied, applied)), "col", "row"
     )
     factor = jnp.linalg.cholesky(energy)
     identity = jnp.eye(vectors, dtype=jnp.float32)

time: 157 us -> 166 us (1.057)
  blocking collectives: 73 us -> 81.6 us
    psum x1 -> x2, blocking collectives: 40 us -> 48.6 us  [the longest x1 37.8 us: by_each_axis(): return lax.psum(half, axis_two)]
where the time goes in v1:
time: 166 us; the launch traced here: 165 us
  blocking collectives  81.6 us (49%)
  local copies, waits for them, and re-layouts  24.5 us (15%)
  waiting for transfers between devices  22.9 us (14%)
  other arithmetic  16.1 us (10%)
  between operations  14.2 us (9%)
  matrix products  5.85 us (4%)
    psum x1, blocking collectives, by_each_axis(): return lax.psum(half, axis_two)  37.8 us
    all_gather x1, blocking collectives, on_device(): gathered = lax.all_gather(scaled, 'row', axis=1, tiled=True)  33 us
    reduce_scatter x1, waiting for transfers between devices, on_device(): lax.psum_scatter(whole_rows, 'col', scatter_dimension=1, tiled=True)  22.9 us
    gather x3, local copies, waits for them, and re-layouts, on_device(): chosen = jnp.take(blocks, pick_index, axis=1)  16.3 us
    psum x1, blocking collectives, by_each_axis(): half = lax.psum(value, axis_one)  10.7 us
    another operation x3, other arithmetic, on_device(): factor = jnp.linalg.cholesky(energy)  6.52 us
    another operation x2, other arithmetic, on_device(): lax.linalg.triangular_solve(factor, identity, left_side=True, lower=True)  5.55 us
    reshape x2, local copies, waits for them, and re-layouts, on_device(): blocks = gathered.reshape(vectors, sources * per_piece, height)  4.01 us
  transfers between devices with their start and end apart: 1, of which 1 were waited for; matrix products, arithmetic and copies ran while one was open for 0% of the time, Pallas kernels for 0%

profile of v1, /device:TPU:0, one launch (start us, length us, event | category | flops | bytes accessed | tf_op | source)
XLA Modules:
  0.0 165.2 jit_solution(10301611805834197570)
XLA Ops:
  7.2 0.9 copy.22
  8.1 0.7 compare_and_fusion
  8.8 0.7 convert_rsqrt_fusion
  9.5 0.9 fusion.8
  10.4 33.0 %all_gather.3 = bf16[64,4096]{1,0:T(8,128)(2,1)S(1)} all-gather(bf16[64,512]{1,0:T(8,128)(2,1)S(1)} %fusion.8), channel_id=1, replica_groups=mesh['row'=8,'col'=4] {'row'}, dimensions={1}, use_global_device_ids=true | all-gather | bytes 589824 | tf_op jit(solution)/shard_map/all_gather | solution.py:35
  43.4 2.1 %reshape.72 = bf16[64,64,64]{2,1,0:T(8,128)(2,1)} reshape(bf16[64,4096]{1,0:T(8,128)(2,1)S(1)} %all_gather.3) | data formatting | bytes 1048576 | tf_op jit(solution)/shard_map/reshape | solution.py:36
  45.5 1.9 %copy.23 = bf16[64,64,64]{2,0,1:T(8,128)(2,1)S(1)} copy(bf16[64,64,64]{2,1,0:T(8,128)(2,1)} %reshape.72) | data formatting | bytes 1048576 | tf_op jit(solution)/shard_map/reshape | solution.py:36
  47.5 3.1 %gather_fusion = bf16[256,64,64]{2,1,0:T(8,128)(2,1)} fusion(bf16[64,64,64]{2,0,1:T(8,128)(2,1)S(1)} %copy.23, s32[1024]{0:T(1024)S(1)} %pad_clamp_fusion), kind=kCustom, calls=%fused_computation | custom fusion | bytes 4195328 | tf_op jit(solution)/shard_map/jit(_take)/gather | solution.py:38
  50.6 6.8 %copy.24 = bf16[64,256,64]{2,1,0:T(8,128)(2,1)} copy(bf16[64,256,64]{2,0,1:T(8,128)(2,1)} %bitcast.30) | data formatting | bytes 4194304 | tf_op jit(solution)/shard_map/jit(_take)/gather | solution.py:38
  57.4 6.5 %gather.7 = bf16[64,32,512]{2,1,0:T(8,128)(2,1)} reshape(bf16[64,256,64]{2,1,0:T(8,128)(2,1)} %copy.24) | data formatting | bytes 4194304 | tf_op jit(solution)/shard_map/jit(_take)/gather | solution.py:38
  63.9 0.1 copy.25
  64.0 0.1 mul.35
  64.1 0.1 mul.36
  64.2 0.1 copy.21
  64.3 0.1 broadcast_in_dim.18
  64.4 0.1 broadcast_in_dim.19
  64.5 1.8 %select_multiply_fusion = bf16[64,32,512]{2,1,0:T(8,128)(2,1)S(1)} fusion(bf16[64,32,512]{2,1,0:T(8,128)(2,1)} %gather.7, pred[32,512]{1,0:T(8,128)(4,1)S(1)} %broadcast_in_dim.19, bf16[32,512]{1,0:T(8,128)(2,1)S(1)} %mul.36), kind=kLoop, calls=%fused_computation.4 | loop fusion | flops 2097152 | bytes 4243456 | tf_op jit(solution)/shard_map/mul | solution.py:39
  66.3 1.4 fusion.3
  67.7 0.6 copy.27
  68.4 1.1 reshape.73
  69.5 22.9 %reduce-scatter.2.cloned.1.call-done = f32[64,512]{1,0:T(8,128)} async-done(((f32[64,2048]{1,0:T(8,128)}), f32[64,512]{1,0:T(8,128)}) %reduce-scatter.2.cloned.1.call-update) | async-done | bytes 131088 | tf_op jit(solution)/shard_map/reduce_scatter | solution.py:44
  92.5 1.1 convolution_bitcast_fusion
  93.6 1.3 fusion.9
  94.8 10.7 %all-reduce.1 = (f32[64,64]{0,1:T(8,128)S(1)}, f32[64,64]{0,1:T(8,128)S(1)}) all-reduce(f32[64,64]{0,1:T(8,128)S(1)} %fusion.9, f32[64,64]{0,1:T(8,128)S(1)} %convolution_bitcast_fusion), channel_id=1, replica_groups=mesh['row'=8,'col'=4] {'col'}, use_global_device_ids=true, to_apply=%region_1.2 | all-reduce | flops 8192 | bytes 65536 | tf_op jit(solution)/shard_map/psum | solution.py:9
  105.6 37.8 %all-reduce = (f32[64,64]{0,1:T(8,128)S(1)}, f32[64,64]{0,1:T(8,128)S(1)}) all-reduce(f32[64,64]{0,1:T(8,128)S(1)} %get-tuple-element.10, f32[64,64]{0,1:T(8,128)S(1)} %get-tuple-element.11), channel_id=1, replica_groups=mesh['row'=8,'col'=4] {'row'}, use_global_device_ids=true, to_apply=%region_2.3 | all-reduce | flops 8192 | bytes 65536 | tf_op jit(solution)/shard_map/psum | solution.py:10
  143.5 5.8 %cholesky.17 = f32[64,64]{1,0:T(8,128)S(1)} custom-call(f32[64,64]{1,0:T(8,128)S(1)} %fusion.16), custom_call_target="Cholesky" | custom-call | tf_op jit(solution)/shard_map/jit(cholesky)/cholesky | solution.py:49
  149.4 0.6 compare_reduce_fusion
  150.0 0.7 fusion.13
  150.7 4.9 %custom-call.6 = f32[1,64,64]{1,2,0:T(8,128)S(1)} custom-call(f32[1,64,64]{2,1,0:T(8,128)S(1)} %fusion.13), custom_call_target="InvertDiagBlocksLowerTriangular" | custom-call | tf_op jit(solution)/shard_map/triangular_solve | solution.py:51
  155.6 0.2 fusion.14
  155.8 0.7 copy.30
  156.5 1.8 %convolution_multiply_fusion = f32[64,512]{1,0:T(8,128)} fusion(f32[64,64]{1,0:T(8,128)S(1)} %fusion.14, bf16[64,512]{1,0:T(8,128)(2,1)S(1)} %copy-done.1, f32[64,512]{1,0:T(8,128)} %reduce-scatter.2.cloned.1.call-done, f32[512]{0:T(512)S(1)} %convert_rsqrt_fusion), kind=kOutput, calls=%fused_computation.6 | convolution fusion | flops 25296896 | bytes 346112 | tf_op jit(solution)/shard_map/dot_general | solution.py:53
  (16 shorter events, 0.3 us)
Async XLA Ops:
  7.2 59.1 %copy-start = (bf16[32,1,64,512]{3,2,1,0:T(8,128)(2,1)S(1)}, bf16[32,1,64,512]{3,2,1,0:T(8,128)(2,1)}, u32[]{:S(2)}) copy-start(bf16[32,1,64,512]{3,2,1,0:T(8,128)(2,1)} %param.7) | copy-start | bytes 6291460
  7.2 85.3 %reduce-scatter.2.cloned.1.call-start = ((), (), s32[]{:S(2)}) async-start(), calls=%async_computation.1 | async-start | bytes 655360 | tf_op jit(solution)/shard_map/reduce_scatter | solution.py:44
  57.4 6.5 %copy-start.2 = (s32[32,1,8]{0,2,1:T(8,128)S(1)}, s32[32,1,8]{0,2,1:T(8,128)}, u32[]{:S(2)}) copy-start(s32[32,1,8]{0,2,1:T(8,128)} %param.9) | copy-start | bytes 3076
  67.7 24.7 %copy-start.1 = (bf16[64,512]{1,0:T(8,128)(2,1)S(1)}, bf16[64,512]{1,0:T(8,128)(2,1)}, u32[]{:S(2)}) copy-start(bf16[64,512]{1,0:T(8,128)(2,1)} %param.5) | copy-start | bytes 196612
Sparse Core Ops, SparseCore 0:
  69.7 22.7 reduce-scatter.1
